TPU v7x, 32 devices: a whole 2x2x4 slice. The times are simulated.
32 devices in a mesh: leaf: 4 (over y, x), col: 8 (over z, core).
Axes of the slice: x: 2, y: 2, z: 4, core: 2. Of those that a mesh axis runs over, the one named last changes fastest.
Arguments:
- s_blocks: bfloat16 [64, 8, 128, 128], P(('leaf', 'col')), may hold values from -0.0059814453 to 0.0059814453
- z_blocks: bfloat16 [64, 8, 128, 128], P(('leaf', 'col')), may hold values from -1.5 to 1.5
- s_requests: int32 [4, 8, 8, 1], P('leaf', 'col'), may hold values from -1 to 15, as said below
- y_pairs: int32 [64, 8, 8], P(('leaf', 'col')), may hold values from -1 to 7, as said below
- zt_requests: int32 [4, 8, 8, 1], P('leaf', 'col'), may hold values from -1 to 31, as said below
- d_pairs: int32 [64, 8, 8], P(('leaf', 'col')), may hold values from -1 to 7, as said below
- d_requests: int32 [4, 8, 8, 1], P('leaf', 'col'), may hold values from -1 to 31, as said below
- e_pairs: int32 [64, 8, 8], P(('leaf', 'col')), may hold values from -1 to 7, as said below
- z_requests: int32 [4, 8, 8, 1], P('leaf', 'col'), may hold values from -1 to 31, as said below
- z_pairs: int32 [64, 8, 8], P(('leaf', 'col')), may hold values from -1 to 7, as said below
Outputs:
- z_refined: bfloat16 [64, 8, 128, 128], P(('leaf', 'col'))
Inputs may be any that keep to these rules, and one draw needn't show every extreme that they name: `s_requests`: entry [l, c, p, q] is -1 or a slot of the S holdings of the device (l, p); the entries of one [l, c, p] are distinct. Every reader has some peer with all 1 entries used, and one reader uses all entries. `zt_requests`: entry [l, c, p, q] is -1 or a slot of the Z holdings of the device (l, p); the entries of one [l, c, p] are distinct. Every reader has some peer with all 1 entries used, and one reader uses all entries. `d_requests`: entry [l, c, p, q] is -1 or a slot of the D holdings of the device (l, p); the entries of one [l, c, p] are distinct. Every reader has some peer with all 1 entries used, and one reader uses all entries. `z_requests`: entry [l, c, p, q] is -1 or a slot of the Z holdings of the device (l, p); the entries of one [l, c, p] are distinct. Every reader has some peer with all 1 entries used, and one reader uses all entries. `y_pairs`: each entry is -1 or the position p + q of an entry of s_requests that is not -1, for the reader holding the column; every such entry is named at least once. `d_pairs`: each entry is -1 or the position p + q of an entry of zt_requests that is not -1, for the reader holding the column; every such entry is named at least once. `e_pairs`: each entry is -1 or the position p + q of an entry of d_requests that is not -1, for the reader holding the column; every such entry is named at least once. `z_pairs`: each entry is -1 or the position p + q of an entry of z_requests that is not -1, for the reader holding the column; every such entry is named at least once.
All inputs are finite; a program needn't handle non-finite values.
Results may differ from a plain program's by a relative error of at most 0.0059.
Values may be sent and summed in bfloat16 or wider, within the bound.
A program may use at most 64 MiB of HBM per device.

v0:
```python
import functools

import jax
import jax.numpy as jnp
from jax import lax
from jax.experimental import pallas as pl
from jax.experimental.pallas import tpu as pltpu
from jax.sharding import PartitionSpec as P

MESH = pl.DeviceIdType.MESH
S, T, Z, D = range(4)


def kernel(
    n,
    cap,
    cols,
    slots,
    s_asks,
    t_asks,
    z_asks,
    d_asks,
    y_names,
    d_names,
    e_names,
    z_names,
    s_hbm,
    z_hbm,
    out_ref,
    req_ref,
    allreq,
    y_pairs,
    d_pairs,
    e_pairs,
    z_pairs,
    s_ref,
    z_ref,
    send_s,
    send_t,
    send_z,
    send_d,
    xs_t,
    xs_z,
    xs_d,
    xr_t,
    xr_z,
    xr_d,
    f_s,
    f_t,
    f_z,
    f_d,
    y_ref,
    d_ref,
    e_ref,
    req_send,
    req_recv,
    own_sem,
    in_sem,
    z_send,
    z_recv,
    x_send,
    x_recv,
):
    leaf = lax.axis_index("leaf")
    me = lax.axis_index("col")
    partner = leaf + 1 - 2 * lax.rem(leaf, 2)
    hold = cols * slots
    size = z_ref.shape[1]
    fetch = n * cap
    pairs = {S: y_pairs, T: d_pairs, D: e_pairs, Z: z_pairs}
    asks = (s_asks, t_asks, z_asks, d_asks)
    moves = [(a, req_ref.at[pl.ds(kind, 1)]) for kind, a in enumerate(asks)]
    moves += [(s_hbm, s_ref), (z_hbm, z_ref)]
    moves += [(y_names, y_pairs), (d_names, d_pairs), (e_names, e_pairs), (z_names, z_pairs)]
    loads = [pltpu.make_async_copy(a, b, in_sem.at[i]) for i, (a, b) in enumerate(moves)]
    sends = {S: send_s, T: send_t, Z: send_z, D: send_d}
    fetched = {S: f_s, T: f_t, Z: f_z, D: f_d}
    xsends = {T: xs_t, Z: xs_z, D: xs_d}
    xrecvs = {T: xr_t, Z: xr_z, D: xr_d}

    def loop(count, body):
        def step(k, carry):
            body(k)
            return carry

        lax.fori_loop(0, count, step, 0, unroll=n <= 8)

    def at(k):
        if n & (n - 1):
            return lax.rem(me + k, n)
        mask = lax.rem(jnp.int32(n) - k, n)
        total, bit = 0, 1
        while bit < n:
            total += lax.rem(lax.div(me, bit) + lax.div(mask, bit), 2) * bit
            bit *= 2
        return total

    barrier = pltpu.get_barrier_semaphore()

    def greet_own(k):
        pl.semaphore_signal(barrier, inc=1, device_id=(leaf, at(k + 1)), device_id_type=MESH)

    def greet_other(k):
        pl.semaphore_signal(barrier, inc=1, device_id=(partner, at(k)), device_id_type=MESH)

    loop(n - 1, greet_own)
    loop(n, greet_other)
    for load in loads:
        load.start()
    for f in (f_s, f_t, f_z, f_d):
        f[fetch] = jnp.zeros((size, size), f.dtype)
    own_copy = pltpu.make_async_copy(req_ref, allreq.at[me], own_sem)
    for load in loads[:4]:
        load.wait()
    own_copy.start()
    pl.semaphore_wait(barrier, 2 * n - 1)

    def req_copy(side, to_leaf, to, source):
        return pltpu.make_async_remote_copy(
            src_ref=req_ref,
            dst_ref=allreq.at[side * n + source],
            send_sem=req_send.at[side * n + to],
            recv_sem=req_recv.at[side * n + source],
            device_id=(to_leaf, to),
            device_id_type=MESH,
        )

    loop(n - 1, lambda k: req_copy(0, leaf, at(k + 1), me).start())
    loop(n, lambda k: req_copy(1, partner, at(k), me).start())
    own_copy.wait()
    for load in loads[4:6]:
        load.wait()

    def ask(kind, side, c, q):
        return allreq[side * n + c, kind, me * cap + q]

    def x_copy(kind, c):
        span = pl.ds(c * cap, cap)
        return pltpu.make_async_remote_copy(
            src_ref=xsends[kind].at[span],
            dst_ref=xrecvs[kind].at[span],
            send_sem=x_send.at[kind, c],
            recv_sem=x_recv.at[kind, c],
            device_id=(partner, me),
            device_id_type=MESH,
        )

    def z_copy(kind, to, source):
        return pltpu.make_async_remote_copy(
            src_ref=sends[kind].at[pl.ds(to * cap, cap)],
            dst_ref=fetched[kind].at[pl.ds(source * cap, cap)],
            send_sem=z_send.at[kind, to],
            recv_sem=z_recv.at[kind, source],
            device_id=(leaf, to),
            device_id_type=MESH,
        )

    def x_pass(kind, own_ref):
        def body(k):
            c = at(k)
            if kind == T:
                req_copy(1, partner, c, c).wait_recv()
            for q in range(cap):
                slot = jnp.clip(ask(kind, 1, c, q) - hold, 0, hold - 1)
                xsends[kind][c * cap + q] = own_ref[slot]
            x_copy(kind, c).start()

        return body

    def chosen(kind, own_ref, c, q):
        request = ask(kind, 0, c, q)
        block = own_ref[jnp.clip(request, 0, hold - 1)]
        if kind != S:
            block = jnp.where(request < hold, block, xrecvs[kind][c * cap + q])
        if kind == T:
            block = block.T
        return block

    def z_pass(kind, own_ref):
        def body(k):
            c = at(k + 1)
            if kind == S:
                req_copy(0, leaf, c, c).wait_recv()
            else:
                x_copy(kind, c).wait_recv()
            for q in range(cap):
                sends[kind][c * cap + q] = chosen(kind, own_ref, c, q)
            z_copy(kind, c, me).start()

        loop(n - 1, body)
        if kind != S:
            x_copy(kind, me).wait_recv()
        for q in range(cap):
            fetched[kind][me * cap + q] = chosen(kind, own_ref, me, q)

    def arrived(kind):
        loop(n - 1, lambda k: z_copy(kind, at(k + 1), at(k + 1)).wait_recv())

    def x_order(k):
        return lax.rem(k + 1, n)

    def product(kind, local_ref, finish, close=None):
        f = fetched[kind]

        def body(g):
            rhs = local_ref[pl.ds(g * slots, slots)].reshape(slots * size, size)
            for a in range(slots):
                blocks = []
                for b in range(slots):
                    name = pairs[kind][g, a, b]
                    blocks.append(f[jnp.where(name < 0, fetch, name)])
                lhs = jnp.concatenate(blocks, axis=1)
                finish(g * slots + a, a, jnp.dot(lhs, rhs, preferred_element_type=jnp.float32))
            if close is not None:
                close(g)

        lax.fori_loop(0, cols, lambda g, c: (body(g), c)[1], 0, unroll=True)

    def x_start(kind, own_ref):
        body = x_pass(kind, own_ref)
        loop(n, lambda k: body(x_order(k)))

    z_pass(S, s_ref)
    x_start(T, z_ref)
    x_start(Z, z_ref)
    z_pass(T, z_ref)

    for load in loads[6:]:
        load.wait()
    arrived(S)

    def y_finish(i, a, total):
        y_ref[i] = total.astype(y_ref.dtype)

    product(S, z_ref, y_finish)
    z_pass(Z, z_ref)
    arrived(T)

    def d_finish(i, a, total):
        rows = lax.broadcasted_iota(jnp.int32, (size, size), 0)
        columns = lax.broadcasted_iota(jnp.int32, (size, size), 1)
        first = 1.0 if a == 0 else 0.0
        d_ref[i] = (jnp.where(rows == columns, first, 0.0) - total).astype(d_ref.dtype)

    product(T, y_ref, d_finish)
    x_start(D, d_ref)
    z_pass(D, d_ref)
    arrived(D)

    def e_finish(i, a, total):
        e_ref[i] = (0.5 * d_ref[i].astype(jnp.float32) + 0.375 * total).astype(e_ref.dtype)

    product(D, d_ref, e_finish)
    arrived(Z)

    def z_finish(i, a, total):
        out_ref[i] = (z_ref[i].astype(jnp.float32) + total).astype(out_ref.dtype)

    product(Z, e_ref, z_finish)

    loop(n - 1, lambda k: req_copy(0, leaf, at(k + 1), me).wait_send())
    loop(n, lambda k: req_copy(1, partner, at(k), me).wait_send())
    for kind in (S, T, Z, D):
        loop(n - 1, lambda k: z_copy(kind, at(k + 1), me).wait_send())
        if kind != S:
            loop(n, lambda k: x_copy(kind, k).wait_send())


def on_device(
    n,
    s_blocks,
    z_blocks,
    s_requests,
    y_pairs,
    zt_requests,
    d_pairs,
    d_requests,
    e_pairs,
    z_requests,
    z_pairs,
):
    cols, slots, size = z_blocks.shape[:3]
    cap = s_requests.shape[3]
    hold = cols * slots
    flat = (hold, size, size)
    fetch = n * cap
    asks = [
        r.reshape(1, fetch) for r in (s_requests, zt_requests, z_requests, d_requests)
    ]
    names = [y_pairs, d_pairs, e_pairs, z_pairs]
    kind = z_blocks.dtype

    def blocks(count):
        return pltpu.VMEM((count, size, size), kind)

    hbm = pl.BlockSpec(memory_space=pltpu.HBM)
    refined = pl.pallas_call(
        functools.partial(kernel, n, cap, cols, slots),
        out_shape=pltpu.VMEM(flat, kind),
        in_specs=[hbm] * 10,
        out_specs=pl.BlockSpec(memory_space=pltpu.VMEM),
        scratch_shapes=[
            pltpu.SMEM((4, fetch), jnp.int32),
            pltpu.SMEM((2 * n, 4, fetch), jnp.int32),
        ]
        + [pltpu.SMEM(y_pairs.shape, jnp.int32) for _ in range(4)]
        + [blocks(hold) for _ in range(2)]
        + [blocks(fetch) for _ in range(10)]
        + [blocks(fetch + 1) for _ in range(4)]
        + [blocks(hold) for _ in range(3)]
        + [
            pltpu.SemaphoreType.DMA((2 * n,)),
            pltpu.SemaphoreType.DMA((2 * n,)),
            pltpu.SemaphoreType.DMA,
            pltpu.SemaphoreType.DMA((10,)),
            pltpu.SemaphoreType.DMA((4, n)),
            pltpu.SemaphoreType.DMA((4, n)),
            pltpu.SemaphoreType.DMA((4, n)),
            pltpu.SemaphoreType.DMA((4, n)),
        ],
        compiler_params=pltpu.CompilerParams(
            collective_id=0, has_side_effects=True, vmem_limit_bytes=66326528
        ),
    )(*asks, *names, s_blocks.reshape(flat), z_blocks.reshape(flat))
    return refined.reshape(z_blocks.shape)


def solution(mesh):
    flat4 = P(("leaf", "col"), None, None, None)
    flat3 = P(("leaf", "col"), None, None)
    asks = P("leaf", "col", None, None)
    in_specs = (flat4, flat4, asks, flat3, asks, flat3, asks, flat3, asks, flat3)
    return jax.shard_map(
        functools.partial(on_device, mesh.shape["col"]),
        mesh=mesh,
        in_specs=in_specs,
        out_specs=flat4,
        check_vma=False,
    )
```

profile of v0, /device:TPU:0, one launch (start us, length us, event | category | flops | bytes accessed | tf_op | source)
XLA Modules:
  0.0 38.5 jit_solution(9520731450567957956)
XLA Ops:
  0.0 37.7 %shard_map.100 = bf16[16,128,128]{2,1,0:T(8,128)(2,1)S(1)} custom-call(s32[1,8]{1,0:T(1,128)} %bitcast.10, s32[1,8]{1,0:T(1,128)} %bitcast.11, s32[1,8]{1,0:T(1,128)} %bitcast.12, s32[1,8]{1,0:T(1,128)} %bitcast.13, s32[2,8,8]{2,1,0:T(8,128)} %y_names.1, s32[2,8,8]{2,1,0:T(8,128)} %d_names.1, s32[2,8,8]{2,1,0:T(8,128)} %e_names.1, s32[2,8,8]{2,1,0:T(8,128)} %z_names.1, ...), custom_call_target="tpu_custom_call" | custom-call | tf_op jit(solution)/shard_map/pallas_call | solution.py:297
  37.7 0.8 %copy.12 = bf16[2,8,128,128]{3,2,1,0:T(8,128)(2,1)} copy(bf16[2,8,128,128]{3,2,1,0:T(8,128)(2,1)S(1)} %bitcast.7) | data formatting | bytes 1048576
where the time goes:
time: 38.7 us; the launch traced here: 38.5 us
  Pallas kernels  37.7 us (97%)
  local copies, waits for them, and re-layouts  0.8 us (2%)
    pallas_call x1, Pallas kernels, on_device(): pl.pallas_call(functools.partial(kernel, n, cap, cols, slots), out_shape=...  37.7 us
    unnamed x1, local copies, waits for them, and re-layouts  0.8 us

commit v1 on v0

v1 whole, which is shorter than its diff:
```python
import functools

import jax
import jax.numpy as jnp
from jax import lax
from jax.experimental import pallas as pl
from jax.experimental.pallas import tpu as pltpu
from jax.sharding import PartitionSpec as P

MESH = pl.DeviceIdType.MESH
S, T, Z, D = range(4)
OWN, OTHER = range(2)


def kernel(
    n,
    per,
    cap,
    cols,
    slots,
    s_asks,
    t_asks,
    z_asks,
    d_asks,
    y_names,
    d_names,
    e_names,
    z_names,
    s_hbm,
    z_hbm,
    out_ref,
    req_ref,
    allreq,
    y_pairs,
    d_pairs,
    e_pairs,
    z_pairs,
    s_ref,
    z_ref,
    send_s,
    send_t,
    send_z,
    send_d,
    xs_t,
    xs_z,
    xs_d,
    xr_t,
    xr_z,
    xr_d,
    f_s,
    f_t,
    f_z,
    f_d,
    y_ref,
    d_ref,
    e_ref,
    go_sem,
    req_send,
    req_recv,
    in_sem,
    z_send,
    z_recv,
    x_send,
    x_recv,
):
    leaf = lax.axis_index("leaf")
    me = lax.axis_index("col")
    odd = lax.rem(leaf, 2)
    partner = leaf + 1 - 2 * odd
    chips = n // per
    chip = lax.div(me, per)
    hold = cols * slots
    size = z_ref.shape[1]
    fetch = n * cap
    pairs = {S: y_pairs, T: d_pairs, D: e_pairs, Z: z_pairs}
    asks = (s_asks, t_asks, z_asks, d_asks)
    moves = [(a, req_ref.at[pl.ds(kind, 1)]) for kind, a in enumerate(asks)]
    moves += [(s_hbm, s_ref), (z_hbm, z_ref)]
    moves += [(y_names, y_pairs), (d_names, d_pairs), (e_names, e_pairs), (z_names, z_pairs)]
    loads = [pltpu.make_async_copy(a, b, in_sem.at[i]) for i, (a, b) in enumerate(moves)]
    sends = {S: send_s, T: send_t, Z: send_z, D: send_d}
    fetched = {S: f_s, T: f_t, Z: f_z, D: f_d}
    xsends = {T: xs_t, Z: xs_z, D: xs_d}
    xrecvs = {T: xr_t, Z: xr_z, D: xr_d}
    leaves = (leaf, partner)

    def span(low, high, body):
        def step(k, carry):
            body(k)
            return carry

        lax.fori_loop(low, high, step, 0)

    def each_chip(low, high, body):
        def step(k, carry):
            body(k)
            return carry

        lax.fori_loop(low, high, step, 0, unroll=n <= 8)

    barrier = pltpu.get_barrier_semaphore()

    def greet(to_leaf, to):
        pl.semaphore_signal(barrier, inc=1, device_id=(to_leaf, to), device_id_type=MESH)

    def greet_chip(side, c):
        for i in range(per):
            greet(leaves[side], c * per + i)

    def tell_chip(side, c):
        for i in range(per):
            pl.semaphore_signal(
                go_sem.at[side, chip],
                inc=1,
                device_id=(leaves[side], c * per + i),
                device_id_type=MESH,
            )

    for i in range(1, per):
        greet(leaf, chip * per + lax.rem(me + i, per))
    for load in loads:
        load.start()

    @pl.when(odd == 0)
    def _():
        greet_chip(OTHER, chip)

    def greet_up(c):
        greet_chip(OWN, c)
        greet_chip(OTHER, c)

    span(chip + 1, chips, greet_up)
    for f in (f_s, f_t, f_z, f_d):
        f[fetch] = jnp.zeros((size, size), f.dtype)
    pl.semaphore_wait(barrier, per - 1 + per * odd + 2 * per * chip)

    @pl.when(odd == 1)
    def _():
        tell_chip(OTHER, chip)

    def tell_down(k):
        tell_chip(OWN, chip - k)
        tell_chip(OTHER, chip - k)

    span(1, chip + 1, tell_down)
    for load in loads[:4]:
        load.wait()
    own_copy = pltpu.make_async_copy(req_ref, allreq.at[me], req_recv.at[OWN, chip])
    own_copy.start()

    def req_copy(side, to):
        return pltpu.make_async_remote_copy(
            src_ref=req_ref,
            dst_ref=allreq.at[side * n + me],
            send_sem=req_send.at[side],
            recv_sem=req_recv.at[side, chip],
            device_id=(leaves[side], to),
            device_id_type=MESH,
        )

    def ask_chip(side, c):
        for i in range(per):
            req_copy(side, c * per + i).start()

    for i in range(1, per):
        req_copy(OWN, chip * per + lax.rem(me + i, per)).start()

    @pl.when(odd == 1)
    def _():
        ask_chip(OTHER, chip)

    def ask_down(k):
        ask_chip(OWN, chip - k)
        ask_chip(OTHER, chip - k)

    span(1, chip + 1, ask_down)

    @pl.when(odd == 0)
    def _():
        pl.semaphore_wait(go_sem.at[OTHER, chip], per)
        ask_chip(OTHER, chip)

    def ask_up(c):
        for side in (OWN, OTHER):
            pl.semaphore_wait(go_sem.at[side, c], per)
            ask_chip(side, c)

    span(chip + 1, chips, ask_up)
    for load in loads[4:6]:
        load.wait()

    def asked(side, c):
        rows = allreq.at[pl.ds(side * n + c * per, per)]
        pltpu.make_async_remote_copy(
            src_ref=rows,
            dst_ref=rows,
            send_sem=req_send.at[side],
            recv_sem=req_recv.at[side, c],
            device_id=(leaf, me),
            device_id_type=MESH,
        ).wait_recv()

    def ask(kind, side, c, q):
        return allreq[side * n + c, kind, me * cap + q]

    def x_copy(kind, first, count, group):
        part = pl.ds(first * cap, count * cap)
        return pltpu.make_async_remote_copy(
            src_ref=xsends[kind].at[part],
            dst_ref=xrecvs[kind].at[part],
            send_sem=x_send.at[kind],
            recv_sem=x_recv.at[kind, group],
            device_id=(partner, me),
            device_id_type=MESH,
        )

    def z_copy(kind, to):
        return pltpu.make_async_remote_copy(
            src_ref=sends[kind].at[pl.ds(to * cap, cap)],
            dst_ref=fetched[kind].at[pl.ds(me * cap, cap)],
            send_sem=z_send.at[kind],
            recv_sem=z_recv.at[kind],
            device_id=(leaf, to),
            device_id_type=MESH,
        )

    def z_all(kind):
        part = pl.ds(0, (n - 1) * cap)
        return pltpu.make_async_remote_copy(
            src_ref=sends[kind].at[part],
            dst_ref=fetched[kind].at[part],
            send_sem=z_send.at[kind],
            recv_sem=z_recv.at[kind],
            device_id=(leaf, me),
            device_id_type=MESH,
        )

    def x_chip(kind, own_ref, g):
        for i in range(per):
            c = g * per + i
            for q in range(cap):
                slot = jnp.clip(ask(kind, OTHER, c, q) - hold, 0, hold - 1)
                xsends[kind][c * cap + q] = own_ref[slot]
            x_copy(kind, c, 1, g).start()

    def z_chip(kind, own_ref, g):
        if kind != S:
            x_copy(kind, g * per, per, g).wait_recv()
        for i in range(per):
            c = g * per + i
            for q in range(cap):
                request = ask(kind, OWN, c, q)
                block = own_ref[jnp.clip(request, 0, hold - 1)]
                if kind != S:
                    block = jnp.where(request < hold, block, xrecvs[kind][c * cap + q])
                if kind == T:
                    block = block.T
                sends[kind][c * cap + q] = block

            @pl.when(c != me)
            def _(c=c):
                z_copy(kind, c).start()

    def keep(kind):
        for q in range(cap):
            fetched[kind][me * cap + q] = sends[kind][me * cap + q]

    def near(j):
        below = lax.div(chip + chips - j, chips)
        return j + below * (chip - 2 * j)

    def arrived(kind):
        z_all(kind).wait_recv()

    def product(kind, local_ref, finish):
        f = fetched[kind]

        def body(g):
            rhs = local_ref[pl.ds(g * slots, slots)].reshape(slots * size, size)
            for a in range(slots):
                blocks = []
                for b in range(slots):
                    name = pairs[kind][g, a, b]
                    blocks.append(f[jnp.where(name < 0, fetch, name)])
                lhs = jnp.concatenate(blocks, axis=1)
                finish(g * slots + a, a, jnp.dot(lhs, rhs, preferred_element_type=jnp.float32))

        lax.fori_loop(0, cols, lambda g, c: (body(g), c)[1], 0, unroll=True)

    def first(j):
        g = near(j)
        asked(OWN, g)
        z_chip(S, s_ref, g)
        asked(OTHER, g)
        x_chip(T, z_ref, g)

    with jax.named_scope("first"):
        each_chip(0, chips, first)
    with jax.named_scope("xZ"):
        each_chip(0, chips, lambda g: x_chip(Z, z_ref, g))
    with jax.named_scope("zT"):
        each_chip(0, chips, lambda j: z_chip(T, z_ref, near(j)))
        keep(S)
        keep(T)

    for load in loads[6:]:
        load.wait()
    with jax.named_scope("arrS"):
        arrived(S)

    def y_finish(i, a, total):
        y_ref[i] = total.astype(y_ref.dtype)

    with jax.named_scope("pY"):
        product(S, z_ref, y_finish)
    half = (chips + 1) // 2
    with jax.named_scope("zZ1"):
        each_chip(0, half, lambda g: z_chip(Z, z_ref, g))
    with jax.named_scope("arrT"):
        arrived(T)

    def d_finish(i, a, total):
        rows = lax.broadcasted_iota(jnp.int32, (size, size), 0)
        columns = lax.broadcasted_iota(jnp.int32, (size, size), 1)
        one = 1.0 if a == 0 else 0.0
        d_ref[i] = (jnp.where(rows == columns, one, 0.0) - total).astype(d_ref.dtype)

    with jax.named_scope("pD"):
        product(T, y_ref, d_finish)
    with jax.named_scope("xD"):
        each_chip(0, chips, lambda g: x_chip(D, d_ref, g))
    with jax.named_scope("zZ2"):
        each_chip(half, chips, lambda g: z_chip(Z, z_ref, g))
        keep(Z)
    with jax.named_scope("zD"):
        each_chip(0, chips, lambda g: z_chip(D, d_ref, g))
        keep(D)
    with jax.named_scope("arrD"):
        arrived(D)

    def e_finish(i, a, total):
        e_ref[i] = (0.5 * d_ref[i].astype(jnp.float32) + 0.375 * total).astype(e_ref.dtype)

    with jax.named_scope("pE"):
        product(D, d_ref, e_finish)
    with jax.named_scope("arrZ"):
        arrived(Z)

    def z_finish(i, a, total):
        out_ref[i] = (z_ref[i].astype(jnp.float32) + total).astype(out_ref.dtype)

    with jax.named_scope("pO"):
        product(Z, e_ref, z_finish)

    for side in (OWN, OTHER):
        rows = allreq.at[pl.ds(0, n - 1 + side)]
        pltpu.make_async_remote_copy(
            src_ref=rows,
            dst_ref=rows,
            send_sem=req_send.at[side],
            recv_sem=req_recv.at[side, 0],
            device_id=(leaf, me),
            device_id_type=MESH,
        ).wait_send()
    for kind in (S, T, Z, D):
        z_all(kind).wait_send()
        if kind != S:
            x_copy(kind, 0, n, 0).wait_send()


def on_device(
    n,
    s_blocks,
    z_blocks,
    s_requests,
    y_pairs,
    zt_requests,
    d_pairs,
    d_requests,
    e_pairs,
    z_requests,
    z_pairs,
):
    cols, slots, size = z_blocks.shape[:3]
    cap = s_requests.shape[3]
    per = 1 + (n + 1) % 2
    hold = cols * slots
    flat = (hold, size, size)
    fetch = n * cap
    asks = [
        r.reshape(1, fetch) for r in (s_requests, zt_requests, z_requests, d_requests)
    ]
    names = [y_pairs, d_pairs, e_pairs, z_pairs]
    kind = z_blocks.dtype

    def blocks(count):
        return pltpu.VMEM((count, size, size), kind)

    hbm = pl.BlockSpec(memory_space=pltpu.HBM)
    refined = pl.pallas_call(
        functools.partial(kernel, n, per, cap, cols, slots),
        out_shape=pltpu.VMEM(flat, kind),
        in_specs=[hbm] * 10,
        out_specs=pl.BlockSpec(memory_space=pltpu.VMEM),
        scratch_shapes=[
            pltpu.SMEM((4, fetch), jnp.int32),
            pltpu.SMEM((2 * n, 4, fetch), jnp.int32),
        ]
        + [pltpu.SMEM(y_pairs.shape, jnp.int32) for _ in range(4)]
        + [blocks(hold) for _ in range(2)]
        + [blocks(fetch) for _ in range(10)]
        + [blocks(fetch + 1) for _ in range(4)]
        + [blocks(hold) for _ in range(3)]
        + [
            pltpu.SemaphoreType.REGULAR((2, n // per)),
            pltpu.SemaphoreType.DMA((2,)),
            pltpu.SemaphoreType.DMA((2, n // per)),
            pltpu.SemaphoreType.DMA((10,)),
            pltpu.SemaphoreType.DMA((4,)),
            pltpu.SemaphoreType.DMA((4,)),
            pltpu.SemaphoreType.DMA((4,)),
            pltpu.SemaphoreType.DMA((4, n // per)),
        ],
        compiler_params=pltpu.CompilerParams(
            collective_id=0, has_side_effects=True, vmem_limit_bytes=66326528
        ),
    )(*asks, *names, s_blocks.reshape(flat), z_blocks.reshape(flat))
    return refined.reshape(z_blocks.shape)


def solution(mesh):
    flat4 = P(("leaf", "col"), None, None, None)
    flat3 = P(("leaf", "col"), None, None)
    asks = P("leaf", "col", None, None)
    in_specs = (flat4, flat4, asks, flat3, asks, flat3, asks, flat3, asks, flat3)
    return jax.shard_map(
        functools.partial(on_device, mesh.shape["col"]),
        mesh=mesh,
        in_specs=in_specs,
        out_specs=flat4,
        check_vma=False,
    )
```

time: 38.7 us -> 35.4 us (0.915)
  the two profiles are of different devices: /device:TPU:0 before, /device:TPU:29 now
where the time goes in v1:
time: 35.4 us; the launch traced here: 35.2 us
  Pallas kernels  34.4 us (97%)
  local copies, waits for them, and re-layouts  0.8 us (2%)
    pallas_call x1, Pallas kernels, on_device(): pl.pallas_call(functools.partial(kernel, n, per, cap, cols, slots), out_s...  34.4 us
    unnamed x1, local copies, waits for them, and re-layouts  0.8 us

profile of v1, /device:TPU:29, one launch (start us, length us, event | category | flops | bytes accessed | tf_op | source)
XLA Modules:
  0.0 35.2 jit_solution(3608629309670353244)
XLA Ops:
  0.0 34.4 %shard_map.100 = bf16[16,128,128]{2,1,0:T(8,128)(2,1)S(1)} custom-call(s32[1,8]{1,0:T(1,128)} %bitcast.10, s32[1,8]{1,0:T(1,128)} %bitcast.11, s32[1,8]{1,0:T(1,128)} %bitcast.12, s32[1,8]{1,0:T(1,128)} %bitcast.13, s32[2,8,8]{2,1,0:T(8,128)} %y_names.1, s32[2,8,8]{2,1,0:T(8,128)} %d_names.1, s32[2,8,8]{2,1,0:T(8,128)} %e_names.1, s32[2,8,8]{2,1,0:T(8,128)} %z_names.1, ...), custom_call_target="tpu_custom_call" | custom-call | tf_op jit(solution)/shard_map/pallas_call | solution.py:400
  34.4 0.8 %copy.12 = bf16[2,8,128,128]{3,2,1,0:T(8,128)(2,1)} copy(bf16[2,8,128,128]{3,2,1,0:T(8,128)(2,1)S(1)} %bitcast.7) | data formatting | bytes 1048576

commit v2 on v1

--- a/solution.py
+++ b/solution.py
@@ -208,8 +208,8 @@
         return pltpu.make_async_remote_copy(
             src_ref=xsends[kind].at[part],
             dst_ref=xrecvs[kind].at[part],
-            send_sem=x_send.at[kind],
-            recv_sem=x_recv.at[kind, group],
+            send_sem=x_send.at[kind - 1],
+            recv_sem=x_recv.at[kind - 1, group],
             device_id=(partner, me),
             device_id_type=MESH,
         )
@@ -269,6 +269,18 @@
         below = lax.div(chip + chips - j, chips)
         return j + below * (chip - 2 * j)
 
+    half = (chips + 1) // 2
+    turns = list(range(half)) + list(range(half, chips))[::-1]
+
+    def others_first(j):
+        if j == chips - 1:
+            return chip
+        return j + lax.div(j + chips - chip, chips)
+
+    def z_chips(low, high):
+        for j in range(low, high):
+            z_chip(Z, z_ref, turns[j])
+
     def arrived(kind):
         z_all(kind).wait_recv()
 
@@ -297,7 +309,8 @@
     with jax.named_scope("first"):
         each_chip(0, chips, first)
     with jax.named_scope("xZ"):
-        each_chip(0, chips, lambda g: x_chip(Z, z_ref, g))
+        for g in turns:
+            x_chip(Z, z_ref, g)
     with jax.named_scope("zT"):
         each_chip(0, chips, lambda j: z_chip(T, z_ref, near(j)))
         keep(S)
@@ -313,11 +326,11 @@
 
     with jax.named_scope("pY"):
         product(S, z_ref, y_finish)
-    half = (chips + 1) // 2
     with jax.named_scope("zZ1"):
-        each_chip(0, half, lambda g: z_chip(Z, z_ref, g))
+        z_chips(0, half)
     with jax.named_scope("arrT"):
         arrived(T)
+        z_chips(half, half + 1)
 
     def d_finish(i, a, total):
         rows = lax.broadcasted_iota(jnp.int32, (size, size), 0)
@@ -328,12 +341,14 @@
     with jax.named_scope("pD"):
         product(T, y_ref, d_finish)
     with jax.named_scope("xD"):
-        each_chip(0, chips, lambda g: x_chip(D, d_ref, g))
+        for j in range(chips):
+            x_chip(D, d_ref, others_first(j))
     with jax.named_scope("zZ2"):
-        each_chip(half, chips, lambda g: z_chip(Z, z_ref, g))
+        z_chips(half + 1, chips)
         keep(Z)
     with jax.named_scope("zD"):
-        each_chip(0, chips, lambda g: z_chip(D, d_ref, g))
+        for j in range(chips):
+            z_chip(D, d_ref, others_first(j))
         keep(D)
     with jax.named_scope("arrD"):
         arrived(D)
@@ -403,7 +418,7 @@
         in_specs=[hbm] * 10,
         out_specs=pl.BlockSpec(memory_space=pltpu.VMEM),
         scratch_shapes=[
-            pltpu.SMEM((4, fetch), jnp.int32),
+            pltpu.VMEM((4, fetch), jnp.int32),
             pltpu.SMEM((2 * n, 4, fetch), jnp.int32),
         ]
         + [pltpu.SMEM(y_pairs.shape, jnp.int32) for _ in range(4)]
@@ -418,8 +433,8 @@
             pltpu.SemaphoreType.DMA((10,)),
             pltpu.SemaphoreType.DMA((4,)),
             pltpu.SemaphoreType.DMA((4,)),
-            pltpu.SemaphoreType.DMA((4,)),
-            pltpu.SemaphoreType.DMA((4, n // per)),
+            pltpu.SemaphoreType.DMA((3,)),
+            pltpu.SemaphoreType.DMA((3, n // per)),
         ],
         compiler_params=pltpu.CompilerParams(
             collective_id=0, has_side_effects=True, vmem_limit_bytes=66326528

time: 35.4 us -> 34.8 us (0.983)
  the two profiles are of different devices: /device:TPU:29 before, /device:TPU:0 now
where the time goes in v2:
time: 34.8 us; the launch traced here: 34.6 us
  Pallas kernels  33.8 us (97%)
  local copies, waits for them, and re-layouts  0.8 us (2%)
    pallas_call x1, Pallas kernels, on_device(): pl.pallas_call(functools.partial(kernel, n, per, cap, cols, slots), out_s...  33.8 us
    unnamed x1, local copies, waits for them, and re-layouts  0.8 us

profile of v2, /device:TPU:0, one launch (start us, length us, event | category | flops | bytes accessed | tf_op | source)
XLA Modules:
  0.0 34.6 jit_solution(7400916109256703245)
XLA Ops:
  0.0 33.8 %shard_map.100 = bf16[16,128,128]{2,1,0:T(8,128)(2,1)S(1)} custom-call(s32[1,8]{1,0:T(1,128)} %bitcast.10, s32[1,8]{1,0:T(1,128)} %bitcast.11, s32[1,8]{1,0:T(1,128)} %bitcast.12, s32[1,8]{1,0:T(1,128)} %bitcast.13, s32[2,8,8]{2,1,0:T(8,128)} %y_names.1, s32[2,8,8]{2,1,0:T(8,128)} %d_names.1, s32[2,8,8]{2,1,0:T(8,128)} %e_names.1, s32[2,8,8]{2,1,0:T(8,128)} %z_names.1, ...), custom_call_target="tpu_custom_call" | custom-call | tf_op jit(solution)/shard_map/pallas_call | solution.py:415
  33.8 0.8 %copy.12 = bf16[2,8,128,128]{3,2,1,0:T(8,128)(2,1)} copy(bf16[2,8,128,128]{3,2,1,0:T(8,128)(2,1)S(1)} %bitcast.7) | data formatting | bytes 1048576

commit v3 on v2

--- a/solution.py
+++ b/solution.py
@@ -62,6 +62,7 @@
     z_recv,
     x_send,
     x_recv,
+    xd_recv,
 ):
     leaf = lax.axis_index("leaf")
     me = lax.axis_index("col")
@@ -203,13 +204,14 @@
     def ask(kind, side, c, q):
         return allreq[side * n + c, kind, me * cap + q]
 
-    def x_copy(kind, first, count, group):
+    def x_copy(kind, first, count):
         part = pl.ds(first * cap, count * cap)
+        landed = xd_recv.at[first] if kind == D else x_recv.at[kind - 1, lax.div(first, per)]
         return pltpu.make_async_remote_copy(
             src_ref=xsends[kind].at[part],
             dst_ref=xrecvs[kind].at[part],
             send_sem=x_send.at[kind - 1],
-            recv_sem=x_recv.at[kind - 1, group],
+            recv_sem=landed,
             device_id=(partner, me),
             device_id_type=MESH,
         )
@@ -241,13 +243,15 @@
             for q in range(cap):
                 slot = jnp.clip(ask(kind, OTHER, c, q) - hold, 0, hold - 1)
                 xsends[kind][c * cap + q] = own_ref[slot]
-            x_copy(kind, c, 1, g).start()
+            x_copy(kind, c, 1).start()
 
     def z_chip(kind, own_ref, g):
-        if kind != S:
-            x_copy(kind, g * per, per, g).wait_recv()
+        if kind in (T, Z):
+            x_copy(kind, g * per, per).wait_recv()
         for i in range(per):
             c = g * per + i
+            if kind == D:
+                x_copy(kind, c, 1).wait_recv()
             for q in range(cap):
                 request = ask(kind, OWN, c, q)
                 block = own_ref[jnp.clip(request, 0, hold - 1)]
@@ -380,7 +384,7 @@
     for kind in (S, T, Z, D):
         z_all(kind).wait_send()
         if kind != S:
-            x_copy(kind, 0, n, 0).wait_send()
+            x_copy(kind, 0, n).wait_send()
 
 
 def on_device(
@@ -434,7 +438,8 @@
             pltpu.SemaphoreType.DMA((4,)),
             pltpu.SemaphoreType.DMA((4,)),
             pltpu.SemaphoreType.DMA((3,)),
-            pltpu.SemaphoreType.DMA((3, n // per)),
+            pltpu.SemaphoreType.DMA((2, n // per)),
+            pltpu.SemaphoreType.DMA((n,)),
         ],
         compiler_params=pltpu.CompilerParams(
             collective_id=0, has_side_effects=True, vmem_limit_bytes=66326528

time: 34.8 us -> 34.5 us (level)
  no operation moved by 1% of the time
where the time goes in v3:
time: 34.5 us; the launch traced here: 34.3 us
  Pallas kernels  33.5 us (97%)
  local copies, waits for them, and re-layouts  0.8 us (2%)
    pallas_call x1, Pallas kernels, on_device(): pl.pallas_call(functools.partial(kernel, n, per, cap, cols, slots), out_s...  33.5 us
    unnamed x1, local copies, waits for them, and re-layouts  0.8 us

profile of v3, /device:TPU:0, one launch (start us, length us, event | category | flops | bytes accessed | tf_op | source)
XLA Modules:
  0.0 34.3 jit_solution(12757982289210498734)
XLA Ops:
  0.0 33.5 %shard_map.100 = bf16[16,128,128]{2,1,0:T(8,128)(2,1)S(1)} custom-call(s32[1,8]{1,0:T(1,128)} %bitcast.10, s32[1,8]{1,0:T(1,128)} %bitcast.11, s32[1,8]{1,0:T(1,128)} %bitcast.12, s32[1,8]{1,0:T(1,128)} %bitcast.13, s32[2,8,8]{2,1,0:T(8,128)} %y_names.1, s32[2,8,8]{2,1,0:T(8,128)} %d_names.1, s32[2,8,8]{2,1,0:T(8,128)} %e_names.1, s32[2,8,8]{2,1,0:T(8,128)} %z_names.1, ...), custom_call_target="tpu_custom_call" | custom-call | tf_op jit(solution)/shard_map/pallas_call | solution.py:419
  33.5 0.8 %copy.12 = bf16[2,8,128,128]{3,2,1,0:T(8,128)(2,1)} copy(bf16[2,8,128,128]{3,2,1,0:T(8,128)(2,1)S(1)} %bitcast.7) | data formatting | bytes 1048576

commit v4 on v3

--- a/solution.py
+++ b/solution.py
@@ -63,6 +63,8 @@
     x_send,
     x_recv,
     xd_recv,
+    cross_ref,
+    cross_recv,
 ):
     leaf = lax.axis_index("leaf")
     me = lax.axis_index("col")
@@ -245,6 +247,50 @@
                 xsends[kind][c * cap + q] = own_ref[slot]
             x_copy(kind, c, 1).start()
 
+    others = [chip * per + lax.rem(me + i, per) for i in range(1, per)]
+
+    def cross_copy(to):
+        return pltpu.make_async_remote_copy(
+            src_ref=xsends[D].at[pl.ds(to * cap, cap)],
+            dst_ref=cross_ref,
+            send_sem=x_send.at[D - 1],
+            recv_sem=cross_recv,
+            device_id=(partner, to),
+            device_id_type=MESH,
+        )
+
+    def x_own_chip():
+        for to in [me, *others]:
+            for q in range(cap):
+                slot = jnp.clip(ask(D, OTHER, to, q) - hold, 0, hold - 1)
+                xsends[D][to * cap + q] = d_ref[slot]
+            if to is me:
+                x_copy(D, me, 1).start()
+            else:
+                cross_copy(to).start()
+
+    def z_own_chip():
+        for other in others:
+            for q in range(cap):
+                request = ask(D, OWN, other, q)
+                sends[D][other * cap + q] = d_ref[jnp.clip(request, 0, hold - 1)]
+            z_copy(D, other).start()
+
+    def settle():
+        x_copy(D, me, 1).wait_recv()
+        for q in range(cap):
+            request = ask(D, OWN, me, q)
+            block = d_ref[jnp.clip(request, 0, hold - 1)]
+            block = jnp.where(request < hold, block, xrecvs[D][me * cap + q])
+            fetched[D][me * cap + q] = block
+        for other in others:
+            cross_copy(other).wait_recv()
+            for q in range(cap):
+                at = other * cap + q
+                request = allreq[me, D, at]
+                block = jnp.where(request < hold, fetched[D][at], cross_ref[q])
+                fetched[D][at] = block
+
     def z_chip(kind, own_ref, g):
         if kind in (T, Z):
             x_copy(kind, g * per, per).wait_recv()
@@ -277,8 +323,6 @@
     turns = list(range(half)) + list(range(half, chips))[::-1]
 
     def others_first(j):
-        if j == chips - 1:
-            return chip
         return j + lax.div(j + chips - chip, chips)
 
     def z_chips(low, high):
@@ -345,17 +389,19 @@
     with jax.named_scope("pD"):
         product(T, y_ref, d_finish)
     with jax.named_scope("xD"):
-        for j in range(chips):
+        for j in range(chips - 1):
             x_chip(D, d_ref, others_first(j))
+        x_own_chip()
     with jax.named_scope("zZ2"):
         z_chips(half + 1, chips)
         keep(Z)
     with jax.named_scope("zD"):
-        for j in range(chips):
+        z_own_chip()
+        for j in range(chips - 1):
             z_chip(D, d_ref, others_first(j))
-        keep(D)
     with jax.named_scope("arrD"):
         arrived(D)
+        settle()
 
     def e_finish(i, a, total):
         e_ref[i] = (0.5 * d_ref[i].astype(jnp.float32) + 0.375 * total).astype(e_ref.dtype)
@@ -440,6 +486,8 @@
             pltpu.SemaphoreType.DMA((3,)),
             pltpu.SemaphoreType.DMA((2, n // per)),
             pltpu.SemaphoreType.DMA((n,)),
+            blocks(cap),
+            pltpu.SemaphoreType.DMA,
         ],
         compiler_params=pltpu.CompilerParams(
             collective_id=0, has_side_effects=True, vmem_limit_bytes=66326528

time: 34.5 us -> 34.5 us (level); the launches traced: 34.3 us -> 33.9 us
  Pallas kernels: 33.5 us -> 33.1 us
    pallas_call x1, Pallas kernels: 33.5 us -> 33.1 us  [on_device(): pl.pallas_call(functools.partial(kernel, n, per, cap, cols, slots), out_s...]
where the time goes in v4:
time: 34.5 us; the launch traced here: 33.9 us
  Pallas kernels  33.1 us (96%)
  local copies, waits for them, and re-layouts  0.8 us (2%)
    pallas_call x1, Pallas kernels, on_device(): pl.pallas_call(functools.partial(kernel, n, per, cap, cols, slots), out_s...  33.1 us
    unnamed x1, local copies, waits for them, and re-layouts  0.8 us

profile of v4, /device:TPU:0, one launch (start us, length us, event | category | flops | bytes accessed | tf_op | source)
XLA Modules:
  0.0 33.9 jit_solution(1668398983770377720)
XLA Ops:
  0.0 33.1 %shard_map.100 = bf16[16,128,128]{2,1,0:T(8,128)(2,1)S(1)} custom-call(s32[1,8]{1,0:T(1,128)} %bitcast.10, s32[1,8]{1,0:T(1,128)} %bitcast.11, s32[1,8]{1,0:T(1,128)} %bitcast.12, s32[1,8]{1,0:T(1,128)} %bitcast.13, s32[2,8,8]{2,1,0:T(8,128)} %y_names.1, s32[2,8,8]{2,1,0:T(8,128)} %d_names.1, s32[2,8,8]{2,1,0:T(8,128)} %e_names.1, s32[2,8,8]{2,1,0:T(8,128)} %z_names.1, ...), custom_call_target="tpu_custom_call" | custom-call | tf_op jit(solution)/shard_map/pallas_call | solution.py:465
  33.1 0.8 %copy.12 = bf16[2,8,128,128]{3,2,1,0:T(8,128)(2,1)} copy(bf16[2,8,128,128]{3,2,1,0:T(8,128)(2,1)S(1)} %bitcast.7) | data formatting | bytes 1048576

commit v5 on v4

--- a/solution.py
+++ b/solution.py
@@ -121,8 +121,6 @@
 
     for i in range(1, per):
         greet(leaf, chip * per + lax.rem(me + i, per))
-    for load in loads:
-        load.start()
 
     @pl.when(odd == 0)
     def _():
@@ -133,6 +131,8 @@
         greet_chip(OTHER, c)
 
     span(chip + 1, chips, greet_up)
+    for load in loads:
+        load.start()
     for f in (f_s, f_t, f_z, f_d):
         f[fetch] = jnp.zeros((size, size), f.dtype)
     pl.semaphore_wait(barrier, per - 1 + per * odd + 2 * per * chip)
@@ -275,21 +275,6 @@
                 request = ask(D, OWN, other, q)
                 sends[D][other * cap + q] = d_ref[jnp.clip(request, 0, hold - 1)]
             z_copy(D, other).start()
-
-    def settle():
-        x_copy(D, me, 1).wait_recv()
-        for q in range(cap):
-            request = ask(D, OWN, me, q)
-            block = d_ref[jnp.clip(request, 0, hold - 1)]
-            block = jnp.where(request < hold, block, xrecvs[D][me * cap + q])
-            fetched[D][me * cap + q] = block
-        for other in others:
-            cross_copy(other).wait_recv()
-            for q in range(cap):
-                at = other * cap + q
-                request = allreq[me, D, at]
-                block = jnp.where(request < hold, fetched[D][at], cross_ref[q])
-                fetched[D][at] = block
 
     def z_chip(kind, own_ref, g):
         if kind in (T, Z):
@@ -332,6 +317,23 @@
     def arrived(kind):
         z_all(kind).wait_recv()
 
+    def settle():
+        x_copy(D, me, 1).wait_recv()
+        for q in range(cap):
+            request = ask(D, OWN, me, q)
+            block = d_ref[jnp.clip(request, 0, hold - 1)]
+            block = jnp.where(request < hold, block, xrecvs[D][me * cap + q])
+            fetched[D][me * cap + q] = block
+        for other in others:
+            cross_copy(other).wait_recv()
+        arrived(D)
+        for other in others:
+            for q in range(cap):
+                at = other * cap + q
+                request = allreq[me, D, at]
+                block = jnp.where(request < hold, fetched[D][at], cross_ref[q])
+                fetched[D][at] = block
+
     def product(kind, local_ref, finish):
         f = fetched[kind]
 
@@ -400,7 +402,6 @@
         for j in range(chips - 1):
             z_chip(D, d_ref, others_first(j))
     with jax.named_scope("arrD"):
-        arrived(D)
         settle()
 
     def e_finish(i, a, total):

time: 34.5 us -> 34.4 us (level)
  no operation moved by 1% of the time
where the time goes in v5:
time: 34.4 us; the launch traced here: 33.9 us
  Pallas kernels  33.1 us (96%)
  local copies, waits for them, and re-layouts  0.8 us (2%)
    pallas_call x1, Pallas kernels, on_device(): pl.pallas_call(functools.partial(kernel, n, per, cap, cols, slots), out_s...  33.1 us
    unnamed x1, local copies, waits for them, and re-layouts  0.8 us

profile of v5, /device:TPU:0, one launch (start us, length us, event | category | flops | bytes accessed | tf_op | source)
XLA Modules:
  0.0 33.9 jit_solution(15281183822569757928)
XLA Ops:
  0.0 33.1 %shard_map.100 = bf16[16,128,128]{2,1,0:T(8,128)(2,1)S(1)} custom-call(s32[1,8]{1,0:T(1,128)} %bitcast.10, s32[1,8]{1,0:T(1,128)} %bitcast.11, s32[1,8]{1,0:T(1,128)} %bitcast.12, s32[1,8]{1,0:T(1,128)} %bitcast.13, s32[2,8,8]{2,1,0:T(8,128)} %y_names.1, s32[2,8,8]{2,1,0:T(8,128)} %d_names.1, s32[2,8,8]{2,1,0:T(8,128)} %e_names.1, s32[2,8,8]{2,1,0:T(8,128)} %z_names.1, ...), custom_call_target="tpu_custom_call" | custom-call | tf_op jit(solution)/shard_map/pallas_call | solution.py:466
  33.1 0.8 %copy.12 = bf16[2,8,128,128]{3,2,1,0:T(8,128)(2,1)} copy(bf16[2,8,128,128]{3,2,1,0:T(8,128)(2,1)S(1)} %bitcast.7) | data formatting | bytes 1048576
